TPU v7x, 32 devices: a whole 2x2x4 slice. The times are simulated.
32 devices in a mesh: grp: 2 (over core), blk: 16 (over z, y, x).
Axes of the slice: x: 2, y: 2, z: 4, core: 2. Of those that a mesh axis runs over, the one named last changes fastest.
Arguments:
- nullspace: float32 [6, 65536], P(None, ('grp', 'blk')), may hold values from -6 to 6
- agg_ids: int32 [65536], P(('grp', 'blk')), may hold values from 0 to 1535
- nbr_index: int32 [8, 65536], P(None, ('grp', 'blk')), may hold values from 0 to 6143
- nbr_weight: float32 [8, 65536], P(None, ('grp', 'blk')), may hold values from -0.25 to 0.25
Outputs:
- factor: float32 [21, 3072], P(None, ('grp', 'blk'))
- spread: float32 [3072], P(('grp', 'blk'))
All inputs are finite; a program needn't handle non-finite values.
Results may differ from a plain program's by a relative error of at most 0.000088.
Values sent between devices are 32-bit elements; how exact they have to be, the bound alone decides.
No kernel may reach another device: no remote copies, remote signals or barrier semaphores. Data moves between devices by JAX's collectives and lax.ppermute only.
A program may use at most 64 MiB of HBM per device.

v0:
```python
import jax
import jax.numpy as jnp
from jax import lax
from jax.sharding import PartitionSpec as P

ROWS_DEV = 2048
AGG_DEV = 96


def with_halo(cells, sides, width):
    for axis, dim in sides:
        count = lax.axis_size(axis)
        ends = count - 1
        head = lax.slice_in_dim(cells, 0, width, axis=dim)
        tail = lax.slice_in_dim(cells, cells.shape[dim] - width, cells.shape[dim], axis=dim)
        cells = jnp.concatenate(
            [
                lax.ppermute(tail, axis, [(i, (i + 1) % count) for i in range(ends)]),
                cells,
                lax.ppermute(head, axis, [((i + 1) % count, i) for i in range(ends)]),
            ],
            axis=dim,
        )
    return cells


def pair_list():
    return [(p, q) for p in range(6) for q in range(p, 6)]


def factorize(packed):
    pairs = pair_list()
    entry = {}
    for idx, (p, q) in enumerate(pairs):
        entry[p, q] = packed[idx]
        entry[q, p] = packed[idx]
    lower = {}
    for j in range(6):
        total = entry[j, j]
        for k in range(j):
            total = total - lower[j, k] * lower[j, k]
        diag = jnp.sqrt(total)
        lower[j, j] = diag
        for i in range(j + 1, 6):
            total = entry[i, j]
            for k in range(j):
                total = total - lower[i, k] * lower[j, k]
            lower[i, j] = total / diag
    factor = jnp.stack([lower[q, p] for p, q in pairs], axis=0)
    diags = jnp.stack([lower[j, j] for j in range(6)], axis=0)
    spread = jnp.log(jnp.max(diags, axis=0)) - jnp.log(jnp.min(diags, axis=0))
    return (factor, spread)


def shards(nullspace, agg_ids, nbr_index, nbr_weight):
    vectors, rows = nullspace.shape
    neighbours = nbr_index.shape[0]
    padded = with_halo(nullspace[None], (("grp", 0),), 1)
    extended = jnp.transpose(padded, (1, 0, 2)).reshape(vectors, 3 * rows)
    ext_cols = jnp.arange(3 * rows, dtype=jnp.int32)
    blocks_blk = lax.axis_size("blk")
    group_aggs = AGG_DEV * blocks_blk
    block_rows = min(512, rows)
    count_blocks = rows // block_rows
    null_blocks = jnp.transpose(nullspace.reshape(vectors, count_blocks, block_rows), (1, 0, 2))
    index_blocks = jnp.transpose(nbr_index.reshape(neighbours, count_blocks, block_rows), (1, 0, 2))
    weight_blocks = jnp.transpose(
        nbr_weight.reshape(neighbours, count_blocks, block_rows), (1, 0, 2)
    )
    id_blocks = agg_ids.reshape(count_blocks, block_rows)
    columns = jnp.arange(group_aggs, dtype=jnp.int32)
    pairs = pair_list()

    def accumulate(total, inputs):
        null_part, index_part, weight_part, id_part = inputs
        mixing = jnp.zeros((block_rows, 3 * rows), jnp.float32)
        for k in range(neighbours):
            mixing = mixing + jnp.where(
                index_part[k][:, None] == ext_cols[None, :], weight_part[k][:, None], 0.0
            )
        nearby = lax.dot_general(
            extended,
            mixing,
            (((1,), (1,)), ((), ())),
            precision=lax.Precision.HIGHEST,
            preferred_element_type=jnp.float32,
        )
        smoothed = null_part - nearby
        terms = jnp.stack([smoothed[p] * smoothed[q] for p, q in pairs], axis=0)
        one_hot = (id_part[:, None] == columns[None, :]).astype(jnp.float32)
        total = total + jnp.dot(
            terms, one_hot, precision=lax.Precision.HIGHEST, preferred_element_type=jnp.float32
        )
        return (total, None)

    start_total = jnp.zeros((len(pairs), group_aggs), jnp.float32)
    partial_gram, _ = lax.scan(
        accumulate, start_total, (null_blocks, index_blocks, weight_blocks, id_blocks)
    )
    whole = lax.psum(partial_gram, "blk")
    offset = lax.axis_index("blk") * AGG_DEV
    mine = lax.dynamic_slice_in_dim(whole, offset, AGG_DEV, 1)
    identity = jnp.array([1.0 if p == q else 0.0 for p, q in pairs], jnp.float32)
    gram = mine * (AGG_DEV / ROWS_DEV) + identity[:, None]
    return factorize(gram)


def solution(mesh):
    return jax.shard_map(
        shards,
        mesh=mesh,
        in_specs=(
            P(None, ("grp", "blk")),
            P(("grp", "blk")),
            P(None, ("grp", "blk")),
            P(None, ("grp", "blk")),
        ),
        out_specs=(P(None, ("grp", "blk")), P(("grp", "blk"))),
        check_vma=False,
    )
```

profile of v0, /device:TPU:0, one launch (start us, length us, event | category | flops | bytes accessed | tf_op | source)
XLA Modules:
  0.0 279.0 jit_solution(1921388014540714053)
XLA Ops:
  7.2 2.4 collective-permute-start
  9.6 1.3 collective-permute-start.1
  10.9 0.7 reshape.96
  11.6 1.3 collective-permute-done.1
  13.0 0.9 pad_maximum_fusion
  13.9 145.3 %while.12 = (s32[]{:T(128)}, f32[21,1536]{1,0:T(8,128)S(1)}, f32[4,6,512]{2,1,0:T(8,128)}, s32[4,8,512]{2,1,0:T(8,128)}, f32[4,8,512]{2,1,0:T(8,128)}, /*index=5...) while((s32[]{:T(128)}, f32[21,1536]{1,0:T(8,128)S(1)}, ...), condition=%wide.region_1.2_spmd.clone.clone, body=%wide.region_0.1_spmd.clone.clone.sunk | while | flops 497889792 | bytes 25895224 | solution.py:97
  13.9 1.0 constant_dynamic-slice_fusion.20
  14.9 1.0 constant_dynamic-slice_fusion.21
  16.0 21.4 %fusion.81 = f32[512,6144]{1,0:T(8,128)S(1)} fusion(f32[512]{0:T(512)S(1)} %bitcast.100, s32[512]{0:T(512)S(1)} %bitcast.108, f32[512]{0:T(512)S(1)} %bitcast.94, s32[512]{0:T(512)S(1)} %bitcast.102, f32[512]{0:T(512)S(1)} %bitcast.95, s32[512]{0:T(512)S(1)} %bitcast.103, f32[512]{0:T(512)S(1)} %bitcast.96, ...), kind=kLoop, calls=%fused_computation.11.clone.clone.clone.clone.clone.1.clone.1 | loop fusion | flops 72351744 | bytes 12615680 | tf_op jit(solution)/shard_map/while/body/eval_jaxpr/dot_general | solution.py:81
  37.4 11.4 %fusion.82 = f32[6,512]{1,0:T(8,128)S(1)} fusion(f32[6,6144]{1,0:T(8,128)S(1)} %get-tuple-element.373, f32[4,6,512]{2,1,0:T(8,128)} %get-tuple-element.370, s32[]{:T(128)} %get-tuple-element.352, f32[512,6144]{1,0:T(8,128)S(1)} %fusion.81), kind=kOutput, calls=%fused_computation.48.clone.2 | convolution fusion | flops 226495488 | bytes 12754948 | tf_op jit(solution)/shard_map/while/body/eval_jaxpr/dot_general | solution.py:81
  49.0 1.2 fusion.83
  50.2 1.0 constant_dynamic-slice_fusion.20
  51.2 1.0 constant_dynamic-slice_fusion.21
  52.3 21.4 %fusion.81 = f32[512,6144]{1,0:T(8,128)S(1)} fusion(f32[512]{0:T(512)S(1)} %bitcast.100, s32[512]{0:T(512)S(1)} %bitcast.108, f32[512]{0:T(512)S(1)} %bitcast.94, s32[512]{0:T(512)S(1)} %bitcast.102, f32[512]{0:T(512)S(1)} %bitcast.95, s32[512]{0:T(512)S(1)} %bitcast.103, f32[512]{0:T(512)S(1)} %bitcast.96, ...), kind=kLoop, calls=%fused_computation.11.clone.clone.clone.clone.clone.1.clone.1 | loop fusion | flops 72351744 | bytes 12615680 | tf_op jit(solution)/shard_map/while/body/eval_jaxpr/dot_general | solution.py:81
  73.7 11.4 %fusion.82 = f32[6,512]{1,0:T(8,128)S(1)} fusion(f32[6,6144]{1,0:T(8,128)S(1)} %get-tuple-element.373, f32[4,6,512]{2,1,0:T(8,128)} %get-tuple-element.370, s32[]{:T(128)} %get-tuple-element.352, f32[512,6144]{1,0:T(8,128)S(1)} %fusion.81), kind=kOutput, calls=%fused_computation.48.clone.2 | convolution fusion | flops 226495488 | bytes 12754948 | tf_op jit(solution)/shard_map/while/body/eval_jaxpr/dot_general | solution.py:81
  85.3 1.2 fusion.83
  86.5 1.0 constant_dynamic-slice_fusion.20
  87.6 1.0 constant_dynamic-slice_fusion.21
  88.6 21.4 %fusion.81 = f32[512,6144]{1,0:T(8,128)S(1)} fusion(f32[512]{0:T(512)S(1)} %bitcast.100, s32[512]{0:T(512)S(1)} %bitcast.108, f32[512]{0:T(512)S(1)} %bitcast.94, s32[512]{0:T(512)S(1)} %bitcast.102, f32[512]{0:T(512)S(1)} %bitcast.95, s32[512]{0:T(512)S(1)} %bitcast.103, f32[512]{0:T(512)S(1)} %bitcast.96, ...), kind=kLoop, calls=%fused_computation.11.clone.clone.clone.clone.clone.1.clone.1 | loop fusion | flops 72351744 | bytes 12615680 | tf_op jit(solution)/shard_map/while/body/eval_jaxpr/dot_general | solution.py:81
  110.0 11.4 %fusion.82 = f32[6,512]{1,0:T(8,128)S(1)} fusion(f32[6,6144]{1,0:T(8,128)S(1)} %get-tuple-element.373, f32[4,6,512]{2,1,0:T(8,128)} %get-tuple-element.370, s32[]{:T(128)} %get-tuple-element.352, f32[512,6144]{1,0:T(8,128)S(1)} %fusion.81), kind=kOutput, calls=%fused_computation.48.clone.2 | convolution fusion | flops 226495488 | bytes 12754948 | tf_op jit(solution)/shard_map/while/body/eval_jaxpr/dot_general | solution.py:81
  121.5 0.1 stack.8
  121.7 1.2 fusion.83
  122.8 1.0 constant_dynamic-slice_fusion.20
  123.9 1.0 constant_dynamic-slice_fusion.21
  124.9 21.4 %fusion.81 = f32[512,6144]{1,0:T(8,128)S(1)} fusion(f32[512]{0:T(512)S(1)} %bitcast.100, s32[512]{0:T(512)S(1)} %bitcast.108, f32[512]{0:T(512)S(1)} %bitcast.94, s32[512]{0:T(512)S(1)} %bitcast.102, f32[512]{0:T(512)S(1)} %bitcast.95, s32[512]{0:T(512)S(1)} %bitcast.103, f32[512]{0:T(512)S(1)} %bitcast.96, ...), kind=kLoop, calls=%fused_computation.11.clone.clone.clone.clone.clone.1.clone.1 | loop fusion | flops 72351744 | bytes 12615680 | tf_op jit(solution)/shard_map/while/body/eval_jaxpr/dot_general | solution.py:81
  146.4 11.4 %fusion.82 = f32[6,512]{1,0:T(8,128)S(1)} fusion(f32[6,6144]{1,0:T(8,128)S(1)} %get-tuple-element.373, f32[4,6,512]{2,1,0:T(8,128)} %get-tuple-element.370, s32[]{:T(128)} %get-tuple-element.352, f32[512,6144]{1,0:T(8,128)S(1)} %fusion.81), kind=kOutput, calls=%fused_computation.48.clone.2 | convolution fusion | flops 226495488 | bytes 12754948 | tf_op jit(solution)/shard_map/while/body/eval_jaxpr/dot_general | solution.py:81
  158.0 1.2 fusion.83
  159.2 0.6 copy-done
  159.9 109.0 %all-reduce.2.cloned.1.call-done = f32[21,1536]{1,0:T(8,128)} async-done(((f32[21,1536]{1,0:T(8,128)}), f32[21,1536]{1,0:T(8,128)}) %all-reduce.2.cloned.1.call-update) | async-done | bytes 129040 | tf_op jit(solution)/shard_map/psum | solution.py:100
  268.8 0.8 multiply_add_fusion
  269.7 0.6 subtract_bitcast_fusion
  270.3 1.8 stack.4
  (26 shorter events, 0.7 us)
Async XLA Ops:
  7.2 261.6 %all-reduce.2.cloned.1.call-start = ((), (), s32[]{:S(2)}) async-start(), calls=%async_computation | async-start | bytes 294912 | tf_op jit(solution)/shard_map/psum | solution.py:100
  7.2 4.4 %collective-permute-start = (f32[1,6,2048]{2,1,0:T(8,128)}, f32[1,6,2048]{2,1,0:T(8,128)S(1)}, u32[]{:S(2)}, u32[]{:S(2)}) collective-permute-start(f32[1,6,2048]{2,1,0:T(8,128)} %bitcast.89), channel_id=1, source_target_pairs={{0,16},{1,17},{2,18},{3,19},{4,20},{5,21},{6,22},{7,23},{8,24},{9,... | collective-permute-start | bytes 147464 | tf_op jit(solution)/shard_map/ppermute | solution.py:18
  9.6 3.4 %collective-permute-start.1 = (f32[1,6,2048]{2,1,0:T(8,128)}, f32[1,6,2048]{2,1,0:T(8,128)S(1)}, u32[]{:S(2)}, u32[]{:S(2)}) collective-permute-start(f32[1,6,2048]{2,1,0:T(8,128)} %bitcast.90), channel_id=1, source_target_pairs={{16,0},{17,1},{18,2},{19,3},{20,4},{21,5},{22,6},{23,7},{24,8},{25... | collective-permute-start | bytes 147464 | tf_op jit(solution)/shard_map/ppermute | solution.py:20
  13.8 255.0 %copy-start.1 = (f32[21]{0:T(128)S(1)}, f32[21]{0:T(128)}, u32[]{:S(2)}) copy-start(f32[21]{0:T(128)} %constant.22.clone) | copy-start | bytes 256
  159.2 0.7 copy-start
Sparse Core Ops, SparseCore 0:
  160.0 108.7 all-reduce.1
where the time goes:
time: 280 us; the launch traced here: 279 us
  waiting for transfers between devices  110 us (39%)
  other arithmetic  88.2 us (32%)
  matrix products  50.4 us (18%)
  between operations  14.1 us (5%)
  local copies, waits for them, and re-layouts  12 us (4%)
  starting transfers between devices  3.73 us (1%)
    psum x1, waiting for transfers between devices, shards(): whole = lax.psum(partial_gram, 'blk')  109 us
    dot_general x4, other arithmetic, accumulate(): lax.dot_general(extended, mixing, (((1,), (1,)), ((), ())), precision=lax...  85.7 us
    dot_general x4, matrix products, accumulate(): lax.dot_general(extended, mixing, (((1,), (1,)), ((), ())), precision=lax...  45.7 us
  transfers between devices with their start and end apart: 3, of which 2 were waited for; matrix products, arithmetic and copies ran while one was open for 0% of the time, Pallas kernels for 0%

commit v1 on v0

--- a/solution.py
+++ b/solution.py
@@ -97,7 +97,7 @@
     partial_gram, _ = lax.scan(
         accumulate, start_total, (null_blocks, index_blocks, weight_blocks, id_blocks)
     )
-    whole = lax.psum(partial_gram, "blk")
+    whole = jnp.sum(lax.all_gather(partial_gram, "blk"), axis=0)
     offset = lax.axis_index("blk") * AGG_DEV
     mine = lax.dynamic_slice_in_dim(whole, offset, AGG_DEV, 1)
     identity = jnp.array([1.0 if p == q else 0.0 for p, q in pairs], jnp.float32)

time: 280 us -> 237 us (0.85)
  waiting for transfers between devices: 110 us -> 65.8 us
    psum x1 -> x0, waiting for transfers between devices: 109 us -> none  [shards(): whole = lax.psum(partial_gram, 'blk')]
    all_gather x0 -> x1, waiting for transfers between devices: none -> 64.4 us  [shards(): whole = jnp.sum(lax.all_gather(partial_gram, 'blk'), axis=0)]
where the time goes in v1:
time: 237 us; the launch traced here: 236 us
  other arithmetic  89.3 us (38%)
  waiting for transfers between devices  65.8 us (28%)
  matrix products  50.4 us (21%)
  between operations  14.1 us (6%)
  local copies, waits for them, and re-layouts  12.2 us (5%)
  starting transfers between devices  3.73 us (2%)
    dot_general x4, other arithmetic, accumulate(): lax.dot_general(extended, mixing, (((1,), (1,)), ((), ())), precision=lax...  85.7 us
    all_gather x1, waiting for transfers between devices, shards(): whole = jnp.sum(lax.all_gather(partial_gram, 'blk'), axis=0)  64.4 us
    dot_general x4, matrix products, accumulate(): lax.dot_general(extended, mixing, (((1,), (1,)), ((), ())), precision=lax...  45.7 us
  transfers between devices with their start and end apart: 3, of which 2 were waited for; matrix products, arithmetic and copies ran while one was open for 0% of the time, Pallas kernels for 0%

profile of v1, /device:TPU:0, one launch (start us, length us, event | category | flops | bytes accessed | tf_op | source)
XLA Modules:
  0.0 235.7 jit_solution(7281623664416244246)
XLA Ops:
  7.2 2.4 %collective-permute-start = (f32[1,6,2048]{2,1,0:T(8,128)}, f32[1,6,2048]{2,1,0:T(8,128)S(1)}, u32[]{:S(2)}, u32[]{:S(2)}) collective-permute-start(f32[1,6,2048]{2,1,0:T(8,128)} %bitcast.90), channel_id=1, source_target_pairs={{0,16},{1,17},{2,18},{3,19},{4,20},{5,21},{6,22},{7,23},{8,24},{9,... | collective-permute-start | bytes 147464 | tf_op jit(solution)/shard_map/ppermute | solution.py:18
  9.6 1.3 collective-permute-start.1
  10.9 0.7 reshape.96
  11.6 1.3 collective-permute-done.1
  13.0 0.9 pad_maximum_fusion
  13.9 145.5 %while.12 = (s32[]{:T(128)}, f32[21,1536]{1,0:T(8,128)S(1)}, f32[4,6,512]{2,1,0:T(8,128)}, s32[4,8,512]{2,1,0:T(8,128)}, f32[4,8,512]{2,1,0:T(8,128)}, /*index=5...) while((s32[]{:T(128)}, f32[21,1536]{1,0:T(8,128)S(1)}, ...), condition=%wide.region_1.2_spmd.clone.clone, body=%wide.region_0.1_spmd.clone.clone.sunk | while | flops 497889792 | bytes 25895224 | solution.py:97
  13.9 1.0 constant_dynamic-slice_fusion.20
  14.9 1.0 constant_dynamic-slice_fusion.21
  16.0 21.4 %fusion.81 = f32[512,6144]{1,0:T(8,128)S(1)} fusion(f32[512]{0:T(512)S(1)} %bitcast.101, s32[512]{0:T(512)S(1)} %bitcast.109, f32[512]{0:T(512)S(1)} %bitcast.95, s32[512]{0:T(512)S(1)} %bitcast.103, f32[512]{0:T(512)S(1)} %bitcast.96, s32[512]{0:T(512)S(1)} %bitcast.104, f32[512]{0:T(512)S(1)} %bitcast.97, ...), kind=kLoop, calls=%fused_computation.11.clone.clone.clone.clone.clone.1.clone.1 | loop fusion | flops 72351744 | bytes 12615680 | tf_op jit(solution)/shard_map/while/body/eval_jaxpr/dot_general | solution.py:81
  37.4 11.4 %fusion.82 = f32[6,512]{1,0:T(8,128)S(1)} fusion(f32[6,6144]{1,0:T(8,128)S(1)} %get-tuple-element.373, f32[4,6,512]{2,1,0:T(8,128)} %get-tuple-element.370, s32[]{:T(128)} %get-tuple-element.352, f32[512,6144]{1,0:T(8,128)S(1)} %fusion.81), kind=kOutput, calls=%fused_computation.48.clone.2 | convolution fusion | flops 226495488 | bytes 12754948 | tf_op jit(solution)/shard_map/while/body/eval_jaxpr/dot_general | solution.py:81
  49.0 1.2 fusion.83
  50.2 1.0 constant_dynamic-slice_fusion.20
  51.2 1.0 constant_dynamic-slice_fusion.21
  52.3 21.4 %fusion.81 = f32[512,6144]{1,0:T(8,128)S(1)} fusion(f32[512]{0:T(512)S(1)} %bitcast.101, s32[512]{0:T(512)S(1)} %bitcast.109, f32[512]{0:T(512)S(1)} %bitcast.95, s32[512]{0:T(512)S(1)} %bitcast.103, f32[512]{0:T(512)S(1)} %bitcast.96, s32[512]{0:T(512)S(1)} %bitcast.104, f32[512]{0:T(512)S(1)} %bitcast.97, ...), kind=kLoop, calls=%fused_computation.11.clone.clone.clone.clone.clone.1.clone.1 | loop fusion | flops 72351744 | bytes 12615680 | tf_op jit(solution)/shard_map/while/body/eval_jaxpr/dot_general | solution.py:81
  73.7 11.4 %fusion.82 = f32[6,512]{1,0:T(8,128)S(1)} fusion(f32[6,6144]{1,0:T(8,128)S(1)} %get-tuple-element.373, f32[4,6,512]{2,1,0:T(8,128)} %get-tuple-element.370, s32[]{:T(128)} %get-tuple-element.352, f32[512,6144]{1,0:T(8,128)S(1)} %fusion.81), kind=kOutput, calls=%fused_computation.48.clone.2 | convolution fusion | flops 226495488 | bytes 12754948 | tf_op jit(solution)/shard_map/while/body/eval_jaxpr/dot_general | solution.py:81
  85.2 0.1 stack.8
  85.3 1.2 fusion.83
  86.5 1.0 constant_dynamic-slice_fusion.20
  87.6 1.0 constant_dynamic-slice_fusion.21
  88.6 21.4 %fusion.81 = f32[512,6144]{1,0:T(8,128)S(1)} fusion(f32[512]{0:T(512)S(1)} %bitcast.101, s32[512]{0:T(512)S(1)} %bitcast.109, f32[512]{0:T(512)S(1)} %bitcast.95, s32[512]{0:T(512)S(1)} %bitcast.103, f32[512]{0:T(512)S(1)} %bitcast.96, s32[512]{0:T(512)S(1)} %bitcast.104, f32[512]{0:T(512)S(1)} %bitcast.97, ...), kind=kLoop, calls=%fused_computation.11.clone.clone.clone.clone.clone.1.clone.1 | loop fusion | flops 72351744 | bytes 12615680 | tf_op jit(solution)/shard_map/while/body/eval_jaxpr/dot_general | solution.py:81
  110.0 11.4 %fusion.82 = f32[6,512]{1,0:T(8,128)S(1)} fusion(f32[6,6144]{1,0:T(8,128)S(1)} %get-tuple-element.373, f32[4,6,512]{2,1,0:T(8,128)} %get-tuple-element.370, s32[]{:T(128)} %get-tuple-element.352, f32[512,6144]{1,0:T(8,128)S(1)} %fusion.81), kind=kOutput, calls=%fused_computation.48.clone.2 | convolution fusion | flops 226495488 | bytes 12754948 | tf_op jit(solution)/shard_map/while/body/eval_jaxpr/dot_general | solution.py:81
  121.7 1.2 fusion.83
  122.9 1.0 constant_dynamic-slice_fusion.20
  123.9 1.2 constant_dynamic-slice_fusion.21
  125.1 21.4 %fusion.81 = f32[512,6144]{1,0:T(8,128)S(1)} fusion(f32[512]{0:T(512)S(1)} %bitcast.101, s32[512]{0:T(512)S(1)} %bitcast.109, f32[512]{0:T(512)S(1)} %bitcast.95, s32[512]{0:T(512)S(1)} %bitcast.103, f32[512]{0:T(512)S(1)} %bitcast.96, s32[512]{0:T(512)S(1)} %bitcast.104, f32[512]{0:T(512)S(1)} %bitcast.97, ...), kind=kLoop, calls=%fused_computation.11.clone.clone.clone.clone.clone.1.clone.1 | loop fusion | flops 72351744 | bytes 12615680 | tf_op jit(solution)/shard_map/while/body/eval_jaxpr/dot_general | solution.py:81
  146.5 11.4 %fusion.82 = f32[6,512]{1,0:T(8,128)S(1)} fusion(f32[6,6144]{1,0:T(8,128)S(1)} %get-tuple-element.373, f32[4,6,512]{2,1,0:T(8,128)} %get-tuple-element.370, s32[]{:T(128)} %get-tuple-element.352, f32[512,6144]{1,0:T(8,128)S(1)} %fusion.81), kind=kOutput, calls=%fused_computation.48.clone.2 | convolution fusion | flops 226495488 | bytes 12754948 | tf_op jit(solution)/shard_map/while/body/eval_jaxpr/dot_general | solution.py:81
  158.2 1.2 fusion.83
  159.4 0.6 copy-done
  160.0 64.4 %all-gather.4.cloned.1.call-done = f32[16,21,1536]{2,1,0:T(8,128)} async-done(((f32[1,21,1536]{2,1,0:T(8,128)}), f32[16,21,1536]{2,1,0:T(8,128)}) %all-gather.4.cloned.1.call-update) | async-done | bytes 2064400 | tf_op jit(solution)/shard_map/all_gather | solution.py:100
  224.4 1.8 reduce_sum.9
  226.4 0.6 subtract_bitcast_fusion
  227.0 1.8 stack.4
  (27 shorter events, 0.8 us)
Async XLA Ops:
  7.2 217.3 %all-gather.4.cloned.1.call-start = ((), (), s32[]{:S(2)}) async-start(), calls=%async_computation | async-start | bytes 2506752 | tf_op jit(solution)/shard_map/all_gather | solution.py:100
  7.2 4.4 %collective-permute-start = (f32[1,6,2048]{2,1,0:T(8,128)}, f32[1,6,2048]{2,1,0:T(8,128)S(1)}, u32[]{:S(2)}, u32[]{:S(2)}) collective-permute-start(f32[1,6,2048]{2,1,0:T(8,128)} %bitcast.90), channel_id=1, source_target_pairs={{0,16},{1,17},{2,18},{3,19},{4,20},{5,21},{6,22},{7,23},{8,24},{9,... | collective-permute-start | bytes 147464 | tf_op jit(solution)/shard_map/ppermute | solution.py:18
  9.6 3.4 %collective-permute-start.1 = (f32[1,6,2048]{2,1,0:T(8,128)}, f32[1,6,2048]{2,1,0:T(8,128)S(1)}, u32[]{:S(2)}, u32[]{:S(2)}) collective-permute-start(f32[1,6,2048]{2,1,0:T(8,128)} %bitcast.91), channel_id=1, source_target_pairs={{16,0},{17,1},{18,2},{19,3},{20,4},{21,5},{22,6},{23,7},{24,8},{25... | collective-permute-start | bytes 147464 | tf_op jit(solution)/shard_map/ppermute | solution.py:20
  13.8 212.4 %copy-start.1 = (f32[21]{0:T(128)S(1)}, f32[21]{0:T(128)}, u32[]{:S(2)}) copy-start(f32[21]{0:T(128)} %constant.13.clone) | copy-start | bytes 256
  159.3 0.6 copy-start
Sparse Core Ops, SparseCore 0:
  160.1 64.2 all-gather.3
